TPU v7x, 32 devices: a whole 2x2x4 slice. The times are simulated.
32 devices in a mesh: ctx: 8 (over z, x), chan: 2 (over core), dp: 2 (over y).
Axes of the slice: x: 2, y: 2, z: 4, core: 2. Of those that a mesh axis runs over, the one named last changes fastest.
Arguments:
- q_stream: bfloat16 [2, 2048, 4096], P('dp', 'ctx', 'chan'), may hold values from -6 to 6
- k_stream: bfloat16 [2, 2048, 4096], P('dp', 'ctx', 'chan'), may hold values from -6 to 6
- v_stream: bfloat16 [2, 2048, 4096], P('dp', 'ctx', 'chan'), may hold values from -6 to 6
- out_grad: bfloat16 [2, 2048, 4096], P('dp', 'ctx', 'chan'), may hold values from -6 to 6
- norm_gain: float32 [4096], P('chan'), may hold values from 0.1 to 1.9
- residue: float32 [4096, 16], P('chan'), may hold values from -6 to 6
- rate: float32 [4096, 16], P('chan'), may hold values from -1.5 to 6
Outputs:
- y_out: bfloat16 [2, 2048, 4096], P('dp', 'ctx', 'chan')
- grad_q: bfloat16 [2, 2048, 4096], P('dp', 'ctx', 'chan')
- grad_k: bfloat16 [2, 2048, 4096], P('dp', 'ctx', 'chan')
- grad_v: bfloat16 [2, 2048, 4096], P('dp', 'ctx', 'chan')
- grad_residue: float32 [4096, 16], P('chan')
- grad_rate: float32 [4096, 16], P('chan')
- grad_gain: float32 [4096], P('chan')
All inputs are finite; a program needn't handle non-finite values.
Results may differ from a plain program's by a relative error of at most 0.0051.
Values may be sent and summed in bfloat16 or wider, within the bound.
No kernel may reach another device: no remote copies, remote signals or barrier semaphores. Data moves between devices by JAX's collectives and lax.ppermute only.
A program may use at most 128 MiB of HBM per device.

v0:
```python
import math
import jax
import jax.numpy as jnp
from jax import lax
from jax.sharding import PartitionSpec as P

D = 4096
highest = lax.Precision.HIGHEST
epsilon = 1e-06


def modal(decays, angles, parity, seq_len, with_slope):
    shrink = jnp.exp(-decays)[None, :]
    gap_one = (-jnp.expm1(-decays))[None, :]
    tail_val = jnp.exp(-decays * seq_len)[None, :]
    gap_all = (-jnp.expm1(-decays * seq_len))[None, :]
    odd_rows = (parity > 0)[:, None]
    numer = jnp.where(odd_rows, 1.0 + tail_val, gap_all)
    half_sin = jnp.sin(angles * 0.5)[:, None]
    full_sin = jnp.sin(angles)[:, None]
    den_real = gap_one + 2.0 * shrink * half_sin * half_sin
    den_imag = shrink * full_sin
    magnitude = den_real * den_real + den_imag * den_imag
    value_real = numer * den_real / magnitude
    value_imag = -numer * den_imag / magnitude
    if not with_slope:
        return (value_real, value_imag)
    power = jnp.where(odd_rows, -tail_val, tail_val)
    z_real = shrink * jnp.cos(angles)[:, None]
    z_imag = -shrink * full_sin
    top_real = seq_len * power * den_real - numer * z_real
    top_imag = seq_len * power * den_imag - numer * z_imag
    square_real = den_real * den_real - den_imag * den_imag
    square_imag = 2.0 * den_real * den_imag
    quartic = magnitude * magnitude
    slope_real = (top_real * square_real + top_imag * square_imag) / quartic
    slope_imag = (top_imag * square_real - top_real * square_imag) / quartic
    return (value_real, value_imag, slope_real, slope_imag)


def gating(conv, q_part, grad_part, norm_gain):
    q_float = q_part.astype(jnp.float32)
    grad_float = grad_part.astype(jnp.float32)
    mixed = q_float * conv
    scaled = norm_gain * grad_float
    squares, inner_sum = lax.psum(
        (jnp.sum(mixed * mixed, axis=-1), jnp.sum(scaled * mixed, axis=-1)), "chan"
    )
    inv_rms = lax.rsqrt(squares / D + epsilon)[..., None]
    inner_sum = inner_sum[..., None]
    y_part = (norm_gain * mixed * inv_rms).astype(jnp.bfloat16)
    mixed_grad = inv_rms * scaled - mixed * (inv_rms * inv_rms * inv_rms * inner_sum / D)
    grad_q = (mixed_grad * conv).astype(jnp.bfloat16)
    gate_grad = mixed_grad * q_float
    gain_part = jnp.sum((grad_float * mixed * inv_rms).reshape(-1, conv.shape[-1]), axis=0)
    return (y_part, grad_q, gate_grad, gain_part)


def transform_plan(q_stream, k_stream, v_stream, out_grad, norm_gain, residue, rate):
    ctx_count = lax.axis_size("ctx")
    ctx_rank = lax.axis_index("ctx")
    batch_rows, length, channels = q_stream.shape
    slice_len = length // ctx_count
    seq_len = length * ctx_count
    period = 2 * seq_len
    is_first = ctx_rank == 0
    slots = jnp.arange(ctx_count, dtype=jnp.int32)
    slot_angle = (slots[:, None] * slots[None, :] % (2 * ctx_count)).astype(jnp.float32) * (
        math.pi / ctx_count
    )
    signs = (1 - 2 * (slots % 2)).astype(jnp.float32)
    lead_row = slots[:, None] == 0
    lead_col = slots[None, :] == 0
    forward_real = jnp.where(lead_row, 1.0, jnp.cos(slot_angle))
    forward_imag = jnp.where(lead_row, signs[None, :], -jnp.sin(slot_angle))
    inverse_real = jnp.where(lead_col, 1.0, 2.0 * jnp.cos(slot_angle)) / period
    inverse_imag = jnp.where(lead_col, signs[:, None], -2.0 * jnp.sin(slot_angle)) / period
    columns = jnp.arange(length, dtype=jnp.int32)
    freq_a = jnp.where(is_first, 0, ctx_rank) + 2 * ctx_count * columns
    freq_b = jnp.where(is_first, ctx_count, ctx_rank) + 2 * ctx_count * columns

    def twiddle(freq):
        phase = (freq[:, None] * columns[None, :] % period).astype(jnp.float32) * (
            2.0 * math.pi / period
        )
        return (jnp.cos(phase), jnp.sin(phase))

    cosine_a, sine_a = twiddle(freq_a)
    cosine_b, sine_b = twiddle(freq_b)
    angles_a = freq_a.astype(jnp.float32) * (2.0 * math.pi / period)
    angles_b = freq_b.astype(jnp.float32) * (2.0 * math.pi / period)
    parity_a = freq_a % 2
    parity_b = freq_b % 2

    def spectrum(slices):
        slot_real = jnp.einsum("kb,xbjc->xkjc", forward_real, slices, precision=highest)
        slot_imag = jnp.einsum("kb,xbjc->xkjc", forward_imag, slices, precision=highest)
        rows_real, rows_imag = (
            lax.all_to_all(slot_real, "ctx", split_axis=1, concat_axis=1, tiled=True),
            lax.all_to_all(slot_imag, "ctx", split_axis=1, concat_axis=1, tiled=True),
        )
        rows_real = rows_real.reshape(batch_rows, length, channels)
        rows_imag = rows_imag.reshape(batch_rows, length, channels)
        a_real = jnp.einsum("kj,xjc->xkc", cosine_a, rows_real, precision=highest)
        a_imag = -jnp.einsum("kj,xjc->xkc", sine_a, rows_real, precision=highest)
        b_real = jnp.einsum("kj,xjc->xkc", cosine_b, rows_imag, precision=highest)
        b_imag = -jnp.einsum("kj,xjc->xkc", sine_b, rows_imag, precision=highest)
        return (a_real, a_imag, b_real, b_imag)

    def positions(spec):
        g_ar, g_ai, g_br, g_bi = spec
        u_first = g_ar - g_bi
        u_second = g_ai + g_br
        x_first = jnp.where(is_first, g_ar, u_first)
        x_second = jnp.where(is_first, g_ai, u_second)
        y_first = jnp.where(is_first, g_br, u_second)
        y_second = jnp.where(is_first, -g_bi, u_first)
        out_real = jnp.einsum("kj,xkc->xjc", cosine_a, x_first, precision=highest) - jnp.einsum(
            "kj,xkc->xjc", sine_a, x_second, precision=highest
        )
        out_imag = jnp.einsum("kj,xkc->xjc", cosine_b, y_first, precision=highest) + jnp.einsum(
            "kj,xkc->xjc", sine_b, y_second, precision=highest
        )
        out_real = out_real.reshape(batch_rows, ctx_count, slice_len, channels)
        out_imag = out_imag.reshape(batch_rows, ctx_count, slice_len, channels)
        recv_real, recv_imag = (
            lax.all_to_all(out_real, "ctx", split_axis=1, concat_axis=1, tiled=True),
            lax.all_to_all(out_imag, "ctx", split_axis=1, concat_axis=1, tiled=True),
        )
        return jnp.einsum("bk,xkjc->xbjc", inverse_real, recv_real, precision=highest) + jnp.einsum(
            "bk,xkjc->xbjc", inverse_imag, recv_imag, precision=highest
        )

    def multiply(spec, kernel_rows, flip):
        s_ar, s_ai, s_br, s_bi = spec
        h_ar, h_ai, h_br, h_bi = kernel_rows
        if flip:
            h_ai = -h_ai
            h_bi = -h_bi
        return (
            s_ar * h_ar - s_ai * h_ai,
            s_ai * h_ar + s_ar * h_ai,
            s_br * h_br - s_bi * h_bi,
            s_bi * h_br + s_br * h_bi,
        )

    decays = jnp.exp(rate) / seq_len
    flat_decays = decays.reshape(-1)
    mode_count = residue.shape[1]
    block = math.gcd(length, 64)
    block_count = length // block
    block_ids = jnp.arange(block_count, dtype=jnp.int32)

    def kernel_block(carry, block_index):
        row_start = block_index * block
        pieces_now = []
        for angles, parity in ((angles_a, parity_a), (angles_b, parity_b)):
            angle_rows = lax.dynamic_slice_in_dim(angles, row_start, block)
            parity_rows = lax.dynamic_slice_in_dim(parity, row_start, block)
            f_real, f_imag = modal(flat_decays, angle_rows, parity_rows, seq_len, False)
            pieces_now.append(
                jnp.sum(f_real.reshape(block, channels, mode_count) * residue, axis=-1)
            )
            pieces_now.append(
                jnp.sum(f_imag.reshape(block, channels, mode_count) * residue, axis=-1)
            )
        return (carry, tuple(pieces_now))

    _, kernel_pieces = lax.scan(kernel_block, 0.0, block_ids)
    kernel_rows = tuple((piece.reshape(length, channels) for piece in kernel_pieces))
    value_blocks = (k_stream.astype(jnp.float32) * v_stream.astype(jnp.float32)).astype(
        jnp.bfloat16
    )
    value_sl = lax.all_to_all(
        value_blocks.reshape(batch_rows, ctx_count, slice_len, channels),
        "ctx",
        split_axis=1,
        concat_axis=1,
        tiled=True,
    ).astype(jnp.float32)
    value_spec = spectrum(value_sl)
    conv_sl = positions(multiply(value_spec, kernel_rows, False))
    conv_blk = lax.all_to_all(conv_sl, "ctx", split_axis=1, concat_axis=1, tiled=True).reshape(
        batch_rows, length, channels
    )
    y_out, grad_q, gate_blk, gain_part = gating(conv_blk, q_stream, out_grad, norm_gain)
    gate_sl = lax.all_to_all(
        gate_blk.reshape(batch_rows, ctx_count, slice_len, channels),
        "ctx",
        split_axis=1,
        concat_axis=1,
        tiled=True,
    )
    gate_spec = spectrum(gate_sl)
    grad_sl = positions(multiply(gate_spec, kernel_rows, True))
    value_grad = lax.all_to_all(grad_sl, "ctx", split_axis=1, concat_axis=1, tiled=True).reshape(
        batch_rows, length, channels
    )
    grad_k = (value_grad * v_stream.astype(jnp.float32)).astype(jnp.bfloat16)
    grad_v = (value_grad * k_stream.astype(jnp.float32)).astype(jnp.bfloat16)

    def true_rows(spec):
        s_ar, s_ai, s_br, s_bi = spec
        return (
            jnp.where(is_first, s_ar, s_ar - s_bi),
            jnp.where(is_first, s_ai, s_ai + s_br),
            s_br,
            s_bi,
        )

    z_ar, z_ai, z_br, z_bi = true_rows(value_spec)
    g_ar, g_ai, g_br, g_bi = true_rows(gate_spec)
    cross_ar = jnp.sum(g_ar * z_ar + g_ai * z_ai, axis=0)
    cross_ai = jnp.sum(g_ai * z_ar - g_ar * z_ai, axis=0)
    cross_br = jnp.sum(g_br * z_br + g_bi * z_bi, axis=0)
    cross_bi = jnp.sum(g_bi * z_br - g_br * z_bi, axis=0)
    weight_a = jnp.where(is_first, 1.0, 2.0) / period
    weight_b = jnp.where(is_first, 1.0, 0.0) / period

    def grad_block(totals, block_index):
        row_start = block_index * block
        sums_now = []
        for angles, parity, cross_real, cross_imag in (
            (angles_a, parity_a, cross_ar, cross_ai),
            (angles_b, parity_b, cross_br, cross_bi),
        ):
            angle_rows = lax.dynamic_slice_in_dim(angles, row_start, block)
            parity_rows = lax.dynamic_slice_in_dim(parity, row_start, block)
            real_rows = lax.dynamic_slice_in_dim(cross_real, row_start, block)[:, :, None]
            imag_rows = lax.dynamic_slice_in_dim(cross_imag, row_start, block)[:, :, None]
            f_real, f_imag, d_real, d_imag = modal(
                flat_decays, angle_rows, parity_rows, seq_len, True
            )
            shape_three = (block, channels, mode_count)
            sums_now.append(
                jnp.sum(
                    real_rows * f_real.reshape(shape_three)
                    + imag_rows * f_imag.reshape(shape_three),
                    axis=0,
                )
            )
            sums_now.append(
                jnp.sum(
                    real_rows * d_real.reshape(shape_three)
                    + imag_rows * d_imag.reshape(shape_three),
                    axis=0,
                )
            )
        return (tuple((total + part for total, part in zip(totals, sums_now))), None)

    zero_modes = jnp.zeros((channels, mode_count), jnp.float32)
    (res_a, slope_a, res_b, slope_b), _ = lax.scan(
        grad_block, (zero_modes, zero_modes, zero_modes, zero_modes), block_ids
    )
    res_part = weight_a * res_a + weight_b * res_b
    rate_part = decays * residue * (weight_a * slope_a + weight_b * slope_b)
    return (y_out, grad_q, grad_k, grad_v, res_part, rate_part, gain_part)


def shards(q_stream, k_stream, v_stream, out_grad, norm_gain, residue, rate):
    results = transform_plan(q_stream, k_stream, v_stream, out_grad, norm_gain, residue, rate)
    y_out, grad_q, grad_k, grad_v, res_part, rate_part, gain_part = results
    grad_residue, grad_rate, grad_gain = lax.psum((res_part, rate_part, gain_part), ("ctx", "dp"))
    return (y_out, grad_q, grad_k, grad_v, grad_residue, grad_rate, grad_gain)


def solution(mesh):
    in_specs = (
        P("dp", "ctx", "chan"),
        P("dp", "ctx", "chan"),
        P("dp", "ctx", "chan"),
        P("dp", "ctx", "chan"),
        P("chan"),
        P("chan", None),
        P("chan", None),
    )
    out_specs = (
        P("dp", "ctx", "chan"),
        P("dp", "ctx", "chan"),
        P("dp", "ctx", "chan"),
        P("dp", "ctx", "chan"),
        P("chan", None),
        P("chan", None),
        P("chan"),
    )
    return jax.shard_map(shards, mesh=mesh, in_specs=in_specs, out_specs=out_specs, check_vma=False)
```

profile of v0, /device:TPU:0, one launch (start us, length us, event | category | flops | bytes accessed | tf_op | source)
XLA Modules:
  0.0 1118.8 jit_solution(14108941958894904162)
XLA Ops:
  10.1 7.3 all-to-all-start
  18.8 24.3 %all-to-all-done = bf16[1,8,32,2048]{3,2,0,1:T(8,128)(2,1)S(1)} async-done(((bf16[1,8,32,2048]{3,2,0,1:T(8,128)(2,1)}), bf16[1,8,32,2048]{3,2,0,1:T(8,128)(2,1)S(1)}, u32[]{:S(2)}, u32[]{:S(2)}) %all-to-all-start) | async-done | bytes 1048608 | tf_op jit(solution)/shard_map/all_to_all | solution.py:174
  57.4 41.7 %all-to-all-done.2 = f32[1,8,32,2048]{3,2,0,1:T(8,128)S(1)} async-done(((f32[1,8,32,2048]{3,2,0,1:T(8,128)}), f32[1,8,32,2048]{3,2,0,1:T(8,128)S(1)}, u32[]{:S(2)}, u32[]{:S(2)}) %all-to-all-start.2) | async-done | bytes 2097184 | tf_op jit(solution)/shard_map/all_to_all | solution.py:100
  103.7 114.4 %while.39 = (s32[]{:T(128)}, f32[4,64,2048]{2,1,0:T(8,128)}, f32[4,64,2048]{2,1,0:T(8,128)}, f32[4,64,2048]{2,1,0:T(8,128)}, f32[4,64,2048]{2,1,0:T(8,128)}, /*i...) while((s32[]{:T(128)}, f32[4,64,2048]{2,1,0:T(8,128)}, ...), condition=%wide.region_5.6_spmd, body=%wide.region_0.5_spmd.sunk | while | flops 70910216 | bytes 10621447 | solution.py:169
  115.0 15.1 %fusion.311 = (f32[64,2048]{1,0:T(8,128)S(1)}, f32[64,2048]{1,0:T(8,128)S(1)}, f32[64,2048]{1,0:T(8,128)S(1)}, f32[64,2048]{1,0:T(8,128)S(1)}) fusion(f32[64]{0:T(128)S(1)} %get-tuple-element.922, f32[64]{0:T(128)S(1)} %get-tuple-element.923, f32[2048,16]{0,1:T(8,128)S(1)} %get-tuple-element.1021, f32[2048,16]{0,1:T(8,128)S(1)} %copy.198, ...), kind=kLoop, calls=%fused_computation.19.clone.1 | loop fusion | flops 70778880 | bytes 2884736 | tf_op jit(solution)/shard_map/while/body/eval_jaxpr/reduce_sum | solution.py:165
  143.7 15.1 %fusion.311 = (f32[64,2048]{1,0:T(8,128)S(1)}, f32[64,2048]{1,0:T(8,128)S(1)}, f32[64,2048]{1,0:T(8,128)S(1)}, f32[64,2048]{1,0:T(8,128)S(1)}) fusion(f32[64]{0:T(128)S(1)} %get-tuple-element.922, f32[64]{0:T(128)S(1)} %get-tuple-element.923, f32[2048,16]{0,1:T(8,128)S(1)} %get-tuple-element.1021, f32[2048,16]{0,1:T(8,128)S(1)} %copy.198, ...), kind=kLoop, calls=%fused_computation.19.clone.1 | loop fusion | flops 70778880 | bytes 2884736 | tf_op jit(solution)/shard_map/while/body/eval_jaxpr/reduce_sum | solution.py:165
  172.2 15.1 %fusion.311 = (f32[64,2048]{1,0:T(8,128)S(1)}, f32[64,2048]{1,0:T(8,128)S(1)}, f32[64,2048]{1,0:T(8,128)S(1)}, f32[64,2048]{1,0:T(8,128)S(1)}) fusion(f32[64]{0:T(128)S(1)} %get-tuple-element.922, f32[64]{0:T(128)S(1)} %get-tuple-element.923, f32[2048,16]{0,1:T(8,128)S(1)} %get-tuple-element.1021, f32[2048,16]{0,1:T(8,128)S(1)} %copy.198, ...), kind=kLoop, calls=%fused_computation.19.clone.1 | loop fusion | flops 70778880 | bytes 2884736 | tf_op jit(solution)/shard_map/while/body/eval_jaxpr/reduce_sum | solution.py:165
  200.8 15.1 %fusion.311 = (f32[64,2048]{1,0:T(8,128)S(1)}, f32[64,2048]{1,0:T(8,128)S(1)}, f32[64,2048]{1,0:T(8,128)S(1)}, f32[64,2048]{1,0:T(8,128)S(1)}) fusion(f32[64]{0:T(128)S(1)} %get-tuple-element.922, f32[64]{0:T(128)S(1)} %get-tuple-element.923, f32[2048,16]{0,1:T(8,128)S(1)} %get-tuple-element.1021, f32[2048,16]{0,1:T(8,128)S(1)} %copy.198, ...), kind=kLoop, calls=%fused_computation.19.clone.1 | loop fusion | flops 70778880 | bytes 2884736 | tf_op jit(solution)/shard_map/while/body/eval_jaxpr/reduce_sum | solution.py:165
  241.9 8.5 multiply_subtract_fusion.2
  250.4 9.0 multiply_add_fusion.6
  283.2 37.7 %all-to-all-done.3 = f32[1,8,32,2048]{3,2,0,1:T(8,128)} async-done(((f32[1,8,32,2048]{3,2,0,1:T(8,128)}), f32[1,8,32,2048]{3,2,0,1:T(8,128)}, u32[]{:S(2)}, u32[]{:S(2)}) %all-to-all-start.3) | async-done | bytes 2097184 | tf_op jit(solution)/shard_map/all_to_all | solution.py:127
  331.2 42.2 %all-to-all-done.4 = f32[1,8,32,2048]{3,2,0,1:T(8,128)S(1)} async-done(((f32[1,8,32,2048]{3,2,0,1:T(8,128)}), f32[1,8,32,2048]{3,2,0,1:T(8,128)S(1)}, u32[]{:S(2)}, u32[]{:S(2)}) %all-to-all-start.4) | async-done | bytes 2097184 | tf_op jit(solution)/shard_map/all_to_all | solution.py:128
  379.5 51.9 %all_to_all.60 = f32[1,8,32,2048]{3,2,0,1:T(8,128)S(1)} all-to-all(f32[1,8,32,2048]{3,2,0,1:T(8,128)S(1)} %copy.131), channel_id=1, replica_groups=mesh['ctx'=8,'chan'=2,'dp'=2] {'ctx'}, dimensions={1} | all-to-all | bytes 4194304 | tf_op jit(solution)/shard_map/all_to_all | solution.py:183
  442.2 52.1 %all_to_all.61 = f32[1,8,32,2048]{3,2,0,1:T(8,128)S(1)} all-to-all(f32[1,8,32,2048]{3,2,0,1:T(8,128)S(1)} %bitcast.214), channel_id=1, replica_groups=mesh['ctx'=8,'chan'=2,'dp'=2] {'ctx'}, dimensions={1} | all-to-all | bytes 4194304 | tf_op jit(solution)/shard_map/all_to_all | solution.py:187
  510.3 41.6 %all-to-all-done.8 = f32[1,8,32,2048]{3,2,0,1:T(8,128)} async-done(((f32[1,8,32,2048]{3,2,0,1:T(8,128)}), f32[1,8,32,2048]{3,2,0,1:T(8,128)}, u32[]{:S(2)}, u32[]{:S(2)}) %all-to-all-start.8) | async-done | bytes 2097184 | tf_op jit(solution)/shard_map/all_to_all | solution.py:100
  555.7 7.2 convolution_bitcast_fusion
  562.9 7.3 convolution_bitcast_fusion.1
  570.2 33.8 %all-to-all-done.7 = f32[1,8,32,2048]{3,2,0,1:T(8,128)S(1)} async-done(((f32[1,8,32,2048]{3,2,0,1:T(8,128)}), f32[1,8,32,2048]{3,2,0,1:T(8,128)S(1)}, u32[]{:S(2)}, u32[]{:S(2)}) %all-to-all-start.7) | async-done | bytes 2097184 | tf_op jit(solution)/shard_map/all_to_all | solution.py:99
  609.8 18.4 %subtract_bitcast_fusion.1 = (f32[256,2048]{0,1:T(8,128)}, f32[256,2048]{0,1:T(8,128)}, f32[256,2048]{0,1:T(8,128)}, f32[256,2048]{0,1:T(8,128)}, f32[1,256,2048...) fusion(f32[1,256,2048]{1,2,0:T(8,128)} %copy-done.9, ...), kind=kOutput, calls=%fused_computation.170 | convolution fusion | flops 1630928896 | bytes 41944064 | tf_op jit(solution)/shard_map/kj,xjc->xkc/dot_general | solution.py:104
  650.8 37.5 %all-to-all-done.9 = f32[1,8,32,2048]{3,2,0,1:T(8,128)} async-done(((f32[1,8,32,2048]{3,2,0,1:T(8,128)}), f32[1,8,32,2048]{3,2,0,1:T(8,128)}, u32[]{:S(2)}, u32[]{:S(2)}) %all-to-all-start.9) | async-done | bytes 2097184 | tf_op jit(solution)/shard_map/all_to_all | solution.py:127
  692.8 69.5 %psum.39 = f32[2048]{0:T(1024)} all-reduce(f32[2048]{0:T(1024)S(1)} %get-tuple-element.596), channel_id=1, replica_groups=mesh['ctx'=8,'chan'=2,'dp'=2] {'ctx','dp'}, use_global_device_ids=true, to_apply=%region_19.20 | all-reduce | flops 2048 | bytes 16384 | tf_op jit(solution)/shard_map/psum | solution.py:263
  786.3 7.2 all-to-all-start.11
  794.2 203.1 %while.40 = (s32[]{:T(128)}, f32[2048,16]{0,1:T(8,128)}, f32[2048,16]{0,1:T(8,128)}, f32[2048,16]{0,1:T(8,128)}, f32[2048,16]{0,1:T(8,128)}, /*index=5*/s32[4]{0...) while((s32[]{:T(128)}, f32[2048,16]{0,1:T(8,128)}, ...), condition=%wide.region_15.16_spmd.clone, body=%wide.region_10.15_spmd.clone.sunk | while | flops 180650240 | bytes 40907724 | solution.py:252
  812.7 13.5 %add_reduce_fusion.8 = (f32[2048,16]{0,1:T(8,128)S(1)}, f32[2048,16]{0,1:T(8,128)S(1)}) fusion(f32[64]{0:T(128)S(1)} %get-tuple-element.965, f32[64,2048]{1,0:T(8,128)S(1)} %copy-done, f32[64]{0:T(128)S(1)} %get-tuple-element.966, f32[64]{0:T(128)S(1)} %get-tuple-element.967, f32[64,2048]{1,0:T(8,128)S(1)} %copy-done.1, f32[2048,16]{0,1:T(8,128)S(1)} %copy.203, ...), kind=kLoop, calls=%fused_computation.71.clone.1 | loop fusion | flops 90112000 | bytes 2360128 | tf_op jit(solution)/shard_map/while/body/eval_jaxpr/reduce_sum | solution.py:243
  830.1 12.9 %add_reduce_fusion.7 = (f32[2048,16]{0,1:T(8,128)S(1)}, f32[2048,16]{0,1:T(8,128)S(1)}) fusion(f32[2048,16]{0,1:T(8,128)S(1)} %copy.203, f32[64]{0:T(128)S(1)} %get-tuple-element.954, f32[2048,16]{0,1:T(8,128)S(1)} %copy.204, f32[2048,16]{0,1:T(8,128)S(1)} %copy.205, f32[64,2048]{1,0:T(8,128)S(1)} %constant_dynamic-slice_fusion.8, ...), kind=kLoop, calls=%fused_computation.75.clone.1 | loop fusion | flops 90112000 | bytes 2360128 | tf_op jit(solution)/shard_map/while/body/eval_jaxpr/reduce_sum | solution.py:243
  862.8 13.5 %add_reduce_fusion.8 = (f32[2048,16]{0,1:T(8,128)S(1)}, f32[2048,16]{0,1:T(8,128)S(1)}) fusion(f32[64]{0:T(128)S(1)} %get-tuple-element.965, f32[64,2048]{1,0:T(8,128)S(1)} %copy-done, f32[64]{0:T(128)S(1)} %get-tuple-element.966, f32[64]{0:T(128)S(1)} %get-tuple-element.967, f32[64,2048]{1,0:T(8,128)S(1)} %copy-done.1, f32[2048,16]{0,1:T(8,128)S(1)} %copy.203, ...), kind=kLoop, calls=%fused_computation.71.clone.1 | loop fusion | flops 90112000 | bytes 2360128 | tf_op jit(solution)/shard_map/while/body/eval_jaxpr/reduce_sum | solution.py:243
  881.1 12.9 %add_reduce_fusion.7 = (f32[2048,16]{0,1:T(8,128)S(1)}, f32[2048,16]{0,1:T(8,128)S(1)}) fusion(f32[2048,16]{0,1:T(8,128)S(1)} %copy.203, f32[64]{0:T(128)S(1)} %get-tuple-element.954, f32[2048,16]{0,1:T(8,128)S(1)} %copy.204, f32[2048,16]{0,1:T(8,128)S(1)} %copy.205, f32[64,2048]{1,0:T(8,128)S(1)} %constant_dynamic-slice_fusion.8, ...), kind=kLoop, calls=%fused_computation.75.clone.1 | loop fusion | flops 90112000 | bytes 2360128 | tf_op jit(solution)/shard_map/while/body/eval_jaxpr/reduce_sum | solution.py:243
  913.7 13.5 %add_reduce_fusion.8 = (f32[2048,16]{0,1:T(8,128)S(1)}, f32[2048,16]{0,1:T(8,128)S(1)}) fusion(f32[64]{0:T(128)S(1)} %get-tuple-element.965, f32[64,2048]{1,0:T(8,128)S(1)} %copy-done, f32[64]{0:T(128)S(1)} %get-tuple-element.966, f32[64]{0:T(128)S(1)} %get-tuple-element.967, f32[64,2048]{1,0:T(8,128)S(1)} %copy-done.1, f32[2048,16]{0,1:T(8,128)S(1)} %copy.203, ...), kind=kLoop, calls=%fused_computation.71.clone.1 | loop fusion | flops 90112000 | bytes 2360128 | tf_op jit(solution)/shard_map/while/body/eval_jaxpr/reduce_sum | solution.py:243
  932.0 12.9 %add_reduce_fusion.7 = (f32[2048,16]{0,1:T(8,128)S(1)}, f32[2048,16]{0,1:T(8,128)S(1)}) fusion(f32[2048,16]{0,1:T(8,128)S(1)} %copy.203, f32[64]{0:T(128)S(1)} %get-tuple-element.954, f32[2048,16]{0,1:T(8,128)S(1)} %copy.204, f32[2048,16]{0,1:T(8,128)S(1)} %copy.205, f32[64,2048]{1,0:T(8,128)S(1)} %constant_dynamic-slice_fusion.8, ...), kind=kLoop, calls=%fused_computation.75.clone.1 | loop fusion | flops 90112000 | bytes 2360128 | tf_op jit(solution)/shard_map/while/body/eval_jaxpr/reduce_sum | solution.py:243
  964.6 13.5 %add_reduce_fusion.8 = (f32[2048,16]{0,1:T(8,128)S(1)}, f32[2048,16]{0,1:T(8,128)S(1)}) fusion(f32[64]{0:T(128)S(1)} %get-tuple-element.965, f32[64,2048]{1,0:T(8,128)S(1)} %copy-done, f32[64]{0:T(128)S(1)} %get-tuple-element.966, f32[64]{0:T(128)S(1)} %get-tuple-element.967, f32[64,2048]{1,0:T(8,128)S(1)} %copy-done.1, f32[2048,16]{0,1:T(8,128)S(1)} %copy.203, ...), kind=kLoop, calls=%fused_computation.71.clone.1 | loop fusion | flops 90112000 | bytes 2360128 | tf_op jit(solution)/shard_map/while/body/eval_jaxpr/reduce_sum | solution.py:243
  982.9 12.9 %add_reduce_fusion.7 = (f32[2048,16]{0,1:T(8,128)S(1)}, f32[2048,16]{0,1:T(8,128)S(1)}) fusion(f32[2048,16]{0,1:T(8,128)S(1)} %copy.203, f32[64]{0:T(128)S(1)} %get-tuple-element.954, f32[2048,16]{0,1:T(8,128)S(1)} %copy.204, f32[2048,16]{0,1:T(8,128)S(1)} %copy.205, f32[64,2048]{1,0:T(8,128)S(1)} %constant_dynamic-slice_fusion.8, ...), kind=kLoop, calls=%fused_computation.75.clone.1 | loop fusion | flops 90112000 | bytes 2360128 | tf_op jit(solution)/shard_map/while/body/eval_jaxpr/reduce_sum | solution.py:243
  1004.8 103.6 %all-reduce.3.cloned.1.call-done = (f32[2048,16]{0,1:T(8,128)}, f32[2048,16]{0,1:T(8,128)}) async-done(((f32[2048,16]{0,1:T(8,128)}, f32[2048,16]{0,1:T(8,128)}), (f32[2048,16]{0,1:T(8,128)}, f32[2048,16]{0,1:T(8,128)})) %all-reduce.3.cloned.1.call-update) | async-done | bytes 262160 | tf_op jit(solution)/shard_map/psum | solution.py:263
  (455 shorter events, 330.3 us)
Async XLA Ops:
  10.1 33.0 %all-to-all-start = ((bf16[1,8,32,2048]{3,2,0,1:T(8,128)(2,1)}), bf16[1,8,32,2048]{3,2,0,1:T(8,128)(2,1)S(1)}, u32[]{:S(2)}, u32[]{:S(2)}) async-start(bf16[1,8,32,2048]{3,2,0,1:T(8,128)(2,1)} %bitcast.6), calls=%async_computation | async-start | bytes 2097152 | tf_op jit(solution)/shard_map/all_to_all | solution.py:174
  47.1 52.0 %all-to-all-start.2 = ((f32[1,8,32,2048]{3,2,0,1:T(8,128)}), f32[1,8,32,2048]{3,2,0,1:T(8,128)S(1)}, u32[]{:S(2)}, u32[]{:S(2)}) async-start(f32[1,8,32,2048]{3,2,0,1:T(8,128)} %copy.120), calls=%async_computation.2 | async-start | bytes 4194304 | tf_op jit(solution)/shard_map/all_to_all | solution.py:100
  57.4 46.3 %copy-start.27 = (f32[2048,16]{0,1:T(8,128)S(1)}, f32[2048,16]{0,1:T(8,128)}, u32[]{:S(2)}) copy-start(f32[2048,16]{0,1:T(8,128)} %param.16) | copy-start | bytes 393220
  99.1 136.0 %all-to-all-start.1 = ((f32[1,8,32,2048]{3,2,0,1:T(8,128)}), f32[1,8,32,2048]{3,2,0,1:T(8,128)}, u32[]{:S(2)}, u32[]{:S(2)}) async-start(f32[1,8,32,2048]{3,2,0,1:T(8,128)} %copy.116), calls=%async_computation.1 | async-start | bytes 4194304 | tf_op jit(solution)/shard_map/all_to_all | solution.py:99
  267.5 53.4 %all-to-all-start.3 = ((f32[1,8,32,2048]{3,2,0,1:T(8,128)}), f32[1,8,32,2048]{3,2,0,1:T(8,128)}, u32[]{:S(2)}, u32[]{:S(2)}) async-start(f32[1,8,32,2048]{3,2,0,1:T(8,128)} %bitcast.213), calls=%async_computation.3 | async-start | bytes 4194304 | tf_op jit(solution)/shard_map/all_to_all | solution.py:127
  320.9 52.4 %all-to-all-start.4 = ((f32[1,8,32,2048]{3,2,0,1:T(8,128)}), f32[1,8,32,2048]{3,2,0,1:T(8,128)S(1)}, u32[]{:S(2)}, u32[]{:S(2)}) async-start(f32[1,8,32,2048]{3,2,0,1:T(8,128)} %bitcast.44), calls=%async_computation.4 | async-start | bytes 4194304 | tf_op jit(solution)/shard_map/all_to_all | solution.py:128
  379.4 52.0 %copy-start.25 = (bf16[1,256,2048]{2,1,0:T(8,128)(2,1)S(1)}, bf16[1,256,2048]{2,1,0:T(8,128)(2,1)}, u32[]{:S(2)}) copy-start(bf16[1,256,2048]{2,1,0:T(8,128)(2,1)} %param.11) | copy-start | bytes 3145732
  500.1 51.8 %all-to-all-start.8 = ((f32[1,8,32,2048]{3,2,0,1:T(8,128)}), f32[1,8,32,2048]{3,2,0,1:T(8,128)}, u32[]{:S(2)}, u32[]{:S(2)}) async-start(f32[1,8,32,2048]{3,2,0,1:T(8,128)} %copy.137), calls=%async_computation.8 | async-start | bytes 4194304 | tf_op jit(solution)/shard_map/all_to_all | solution.py:100
  551.9 52.0 %all-to-all-start.7 = ((f32[1,8,32,2048]{3,2,0,1:T(8,128)}), f32[1,8,32,2048]{3,2,0,1:T(8,128)S(1)}, u32[]{:S(2)}, u32[]{:S(2)}) async-start(f32[1,8,32,2048]{3,2,0,1:T(8,128)} %copy.134), calls=%async_computation.7 | async-start | bytes 4194304 | tf_op jit(solution)/shard_map/all_to_all | solution.py:99
  636.0 52.3 %all-to-all-start.9 = ((f32[1,8,32,2048]{3,2,0,1:T(8,128)}), f32[1,8,32,2048]{3,2,0,1:T(8,128)}, u32[]{:S(2)}, u32[]{:S(2)}) async-start(f32[1,8,32,2048]{3,2,0,1:T(8,128)} %bitcast.212), calls=%async_computation.9 | async-start | bytes 4194304 | tf_op jit(solution)/shard_map/all_to_all | solution.py:127
  688.4 89.9 %all-to-all-start.10 = ((f32[1,8,32,2048]{3,2,0,1:T(8,128)}), f32[1,8,32,2048]{3,2,0,1:T(8,128)}, u32[]{:S(2)}, u32[]{:S(2)}) async-start(f32[1,8,32,2048]{3,2,0,1:T(8,128)} %bitcast.211), calls=%async_computation.10 | async-start | bytes 4194304 | tf_op jit(solution)/shard_map/all_to_all | solution.py:128
  786.3 214.4 %all-to-all-start.11 = ((f32[1,8,32,2048]{3,2,0,1:T(8,128)}), f32[1,8,32,2048]{3,2,0,1:T(8,128)}, u32[]{:S(2)}, u32[]{:S(2)}) async-start(f32[1,8,32,2048]{3,2,0,1:T(8,128)} %copy.148), calls=%async_computation.11 | async-start | bytes 4194304 | tf_op jit(solution)/shard_map/all_to_all | solution.py:196
  793.5 314.8 %all-reduce.3.cloned.1.call-start = ((), (), s32[]{:S(2)}) async-start(), calls=%async_computation.12 | async-start | bytes 524288 | tf_op jit(solution)/shard_map/psum | solution.py:263
  812.1 14.2 %copy-start.33 = (f32[2048,16]{0,1:T(8,128)S(1)}, f32[2048,16]{0,1:T(8,128)}, u32[]{:S(2)}) copy-start(f32[2048,16]{0,1:T(8,128)} %get-tuple-element.1055) | copy-start | bytes 393220 | tf_op jit(solution)/shard_map/while
  812.7 14.3 %copy-start.38 = (f32[256]{0:T(256)S(1)}, f32[256]{0:T(256)}, u32[]{:S(2)}) copy-start(f32[256]{0:T(256)} %get-tuple-element.1086) | copy-start | bytes 3076 | tf_op jit(solution)/shard_map/while
  827.7 15.4 %copy-start.29 = (f32[2048,16]{0,1:T(8,128)S(1)}, f32[2048,16]{0,1:T(8,128)}, u32[]{:S(2)}) copy-start(f32[2048,16]{0,1:T(8,128)} %get-tuple-element.1053) | copy-start | bytes 393220 | tf_op jit(solution)/shard_map/while
  827.7 15.4 %copy-start.31 = (f32[2048,16]{0,1:T(8,128)S(1)}, f32[2048,16]{0,1:T(8,128)}, u32[]{:S(2)}) copy-start(f32[2048,16]{0,1:T(8,128)} %get-tuple-element.1054) | copy-start | bytes 393220 | tf_op jit(solution)/shard_map/while
  828.8 15.7 %copy-start.24 = (f32[256,2048]{1,0:T(8,128)S(1)}, f32[256,2048]{1,0:T(8,128)}, u32[]{:S(2)}) copy-start(f32[256,2048]{1,0:T(8,128)} %copy-done.23) | copy-start | bytes 6291460 | tf_op jit(solution)/shard_map/while
  862.1 14.2 %copy-start.33 = (f32[2048,16]{0,1:T(8,128)S(1)}, f32[2048,16]{0,1:T(8,128)}, u32[]{:S(2)}) copy-start(f32[2048,16]{0,1:T(8,128)} %get-tuple-element.1055) | copy-start | bytes 393220 | tf_op jit(solution)/shard_map/while
  862.7 15.2 %copy-start.38 = (f32[256]{0:T(256)S(1)}, f32[256]{0:T(256)}, u32[]{:S(2)}) copy-start(f32[256]{0:T(256)} %get-tuple-element.1086) | copy-start | bytes 3076 | tf_op jit(solution)/shard_map/while
  878.6 15.4 %copy-start.29 = (f32[2048,16]{0,1:T(8,128)S(1)}, f32[2048,16]{0,1:T(8,128)}, u32[]{:S(2)}) copy-start(f32[2048,16]{0,1:T(8,128)} %get-tuple-element.1053) | copy-start | bytes 393220 | tf_op jit(solution)/shard_map/while
  878.6 15.4 %copy-start.31 = (f32[2048,16]{0,1:T(8,128)S(1)}, f32[2048,16]{0,1:T(8,128)}, u32[]{:S(2)}) copy-start(f32[2048,16]{0,1:T(8,128)} %get-tuple-element.1054) | copy-start | bytes 393220 | tf_op jit(solution)/shard_map/while
  879.7 15.7 %copy-start.24 = (f32[256,2048]{1,0:T(8,128)S(1)}, f32[256,2048]{1,0:T(8,128)}, u32[]{:S(2)}) copy-start(f32[256,2048]{1,0:T(8,128)} %copy-done.23) | copy-start | bytes 6291460 | tf_op jit(solution)/shard_map/while
  913.0 14.2 %copy-start.33 = (f32[2048,16]{0,1:T(8,128)S(1)}, f32[2048,16]{0,1:T(8,128)}, u32[]{:S(2)}) copy-start(f32[2048,16]{0,1:T(8,128)} %get-tuple-element.1055) | copy-start | bytes 393220 | tf_op jit(solution)/shard_map/while
  913.7 15.2 %copy-start.38 = (f32[256]{0:T(256)S(1)}, f32[256]{0:T(256)}, u32[]{:S(2)}) copy-start(f32[256]{0:T(256)} %get-tuple-element.1086) | copy-start | bytes 3076 | tf_op jit(solution)/shard_map/while
  929.5 15.4 %copy-start.29 = (f32[2048,16]{0,1:T(8,128)S(1)}, f32[2048,16]{0,1:T(8,128)}, u32[]{:S(2)}) copy-start(f32[2048,16]{0,1:T(8,128)} %get-tuple-element.1053) | copy-start | bytes 393220 | tf_op jit(solution)/shard_map/while
  929.5 15.4 %copy-start.31 = (f32[2048,16]{0,1:T(8,128)S(1)}, f32[2048,16]{0,1:T(8,128)}, u32[]{:S(2)}) copy-start(f32[2048,16]{0,1:T(8,128)} %get-tuple-element.1054) | copy-start | bytes 393220 | tf_op jit(solution)/shard_map/while
  930.6 15.7 %copy-start.24 = (f32[256,2048]{1,0:T(8,128)S(1)}, f32[256,2048]{1,0:T(8,128)}, u32[]{:S(2)}) copy-start(f32[256,2048]{1,0:T(8,128)} %copy-done.23) | copy-start | bytes 6291460 | tf_op jit(solution)/shard_map/while
  964.6 15.2 %copy-start.38 = (f32[256]{0:T(256)S(1)}, f32[256]{0:T(256)}, u32[]{:S(2)}) copy-start(f32[256]{0:T(256)} %get-tuple-element.1086) | copy-start | bytes 3076 | tf_op jit(solution)/shard_map/while
  980.4 15.4 %copy-start.29 = (f32[2048,16]{0,1:T(8,128)S(1)}, f32[2048,16]{0,1:T(8,128)}, u32[]{:S(2)}) copy-start(f32[2048,16]{0,1:T(8,128)} %get-tuple-element.1053) | copy-start | bytes 393220 | tf_op jit(solution)/shard_map/while
  980.4 15.4 %copy-start.31 = (f32[2048,16]{0,1:T(8,128)S(1)}, f32[2048,16]{0,1:T(8,128)}, u32[]{:S(2)}) copy-start(f32[2048,16]{0,1:T(8,128)} %get-tuple-element.1054) | copy-start | bytes 393220 | tf_op jit(solution)/shard_map/while
  981.6 15.7 %copy-start.24 = (f32[256,2048]{1,0:T(8,128)S(1)}, f32[256,2048]{1,0:T(8,128)}, u32[]{:S(2)}) copy-start(f32[256,2048]{1,0:T(8,128)} %copy-done.23) | copy-start | bytes 6291460 | tf_op jit(solution)/shard_map/while
  (63 other events, 244.3 us)
Sparse Core Ops, SparseCore 0:
  1000.8 107.5 all-reduce.2
where the time goes:
time: 1130 us; the launch traced here: 1120 us
  waiting for transfers between devices  362 us (32%)
  other arithmetic  254 us (22%)
  blocking collectives  178 us (16%)
  matrix products  136 us (12%)
  local copies, waits for them, and re-layouts  116 us (10%)
  starting transfers between devices  49.9 us (4%)
  between operations  15 us (1%)
    reduce_sum x8, other arithmetic, grad_block(): jnp.sum(real_rows * d_real.reshape(shape_three) + imag_rows * d_imag.resh...  106 us
    psum x1, waiting for transfers between devices, shards(): lax.psum((res_part, rate_part, gain_part), ('ctx', 'dp'))  104 us
    all_to_all x2, waiting for transfers between devices, spectrum(): lax.all_to_all(slot_imag, 'ctx', split_axis=1, concat_axis=1, tiled=True)  83.3 us
    all_to_all x2, waiting for transfers between devices, positions(): lax.all_to_all(out_real, 'ctx', split_axis=1, concat_axis=1, tiled=True)  75.2 us
    psum x1, blocking collectives, shards(): lax.psum((res_part, rate_part, gain_part), ('ctx', 'dp'))  69.5 us
    reduce_sum x4, other arithmetic, kernel_block(): jnp.sum(f_imag.reshape(block, channels, mode_count) * residue, axis=-1)  60.5 us
    all_to_all x1, blocking collectives, transform_plan(): lax.all_to_all(gate_blk.reshape(batch_rows, ctx_count, slice_len, channel...  52.1 us
    all_to_all x1, blocking collectives, transform_plan(): lax.all_to_all(conv_sl, 'ctx', split_axis=1, concat_axis=1, tiled=True)  51.9 us
  transfers between devices with their start and end apart: 11, of which 8 were waited for; matrix products, arithmetic and copies ran while one was open for 36% of the time, Pallas kernels for 0%

commit v1 on v0

--- a/solution.py
+++ b/solution.py
@@ -260,7 +260,9 @@
 def shards(q_stream, k_stream, v_stream, out_grad, norm_gain, residue, rate):
     results = transform_plan(q_stream, k_stream, v_stream, out_grad, norm_gain, residue, rate)
     y_out, grad_q, grad_k, grad_v, res_part, rate_part, gain_part = results
-    grad_residue, grad_rate, grad_gain = lax.psum((res_part, rate_part, gain_part), ("ctx", "dp"))
+    grad_residue, grad_rate, grad_gain = lax.psum(
+        lax.psum((res_part, rate_part, gain_part), "dp"), "ctx"
+    )
     return (y_out, grad_q, grad_k, grad_v, grad_residue, grad_rate, grad_gain)
 
 

time: 1130 us -> 1080 us (0.956)
  blocking collectives: 178 us -> 137 us
    psum x1 -> x2, blocking collectives: 69.5 us -> 27.7 us  [the longest x1 22.5 us: shards(): lax.psum(lax.psum((res_part, rate_part, gain_part), 'dp'), 'ctx')]
    psum x1 -> x2, waiting for transfers between devices: 104 us -> 68.1 us  [the longest x1 68.1 us: shards(): lax.psum(lax.psum((res_part, rate_part, gain_part), 'dp'), 'ctx')]
    all_to_all x2, waiting for transfers between devices: 42.2 us -> 73.9 us  [positions(): lax.all_to_all(out_imag, 'ctx', split_axis=1, concat_axis=1, tiled=True)]
  transfers between devices with their start and end apart: 11 -> 12, of which waited for: 8 -> 9; matrix products, arithmetic and copies ran while one was open for 36% -> 37% of each run, Pallas kernels for 0% -> 0%
where the time goes in v1:
time: 1080 us; the launch traced here: 1070 us
  waiting for transfers between devices  359 us (33%)
  other arithmetic  254 us (24%)
  blocking collectives  137 us (13%)
  matrix products  136 us (13%)
  local copies, waits for them, and re-layouts  116 us (11%)
  starting transfers between devices  47.3 us (4%)
  between operations  15.1 us (1%)
    reduce_sum x8, other arithmetic, grad_block(): jnp.sum(real_rows * d_real.reshape(shape_three) + imag_rows * d_imag.resh...  106 us
    all_to_all x2, waiting for transfers between devices, spectrum(): lax.all_to_all(slot_imag, 'ctx', split_axis=1, concat_axis=1, tiled=True)  83.3 us
    all_to_all x2, waiting for transfers between devices, positions(): lax.all_to_all(out_real, 'ctx', split_axis=1, concat_axis=1, tiled=True)  75.2 us
    all_to_all x2, waiting for transfers between devices, positions(): lax.all_to_all(out_imag, 'ctx', split_axis=1, concat_axis=1, tiled=True)  73.9 us
    psum x1, waiting for transfers between devices, shards(): lax.psum(lax.psum((res_part, rate_part, gain_part), 'dp'), 'ctx')  68.1 us
    reduce_sum x4, other arithmetic, kernel_block(): jnp.sum(f_imag.reshape(block, channels, mode_count) * residue, axis=-1)  60.5 us
    all_to_all x1, blocking collectives, transform_plan(): lax.all_to_all(gate_blk.reshape(batch_rows, ctx_count, slice_len, channel...  52.1 us
    all_to_all x1, blocking collectives, transform_plan(): lax.all_to_all(conv_sl, 'ctx', split_axis=1, concat_axis=1, tiled=True)  51.9 us
  transfers between devices with their start and end apart: 12, of which 9 were waited for; matrix products, arithmetic and copies ran while one was open for 37% of the time, Pallas kernels for 0%

profile of v1, /device:TPU:0, one launch (start us, length us, event | category | flops | bytes accessed | tf_op | source)
XLA Modules:
  0.0 1071.0 jit_solution(12871189526381682158)
XLA Ops:
  10.1 7.3 all-to-all-start
  18.8 24.3 %all-to-all-done = bf16[1,8,32,2048]{3,2,0,1:T(8,128)(2,1)S(1)} async-done(((bf16[1,8,32,2048]{3,2,0,1:T(8,128)(2,1)}), bf16[1,8,32,2048]{3,2,0,1:T(8,128)(2,1)S(1)}, u32[]{:S(2)}, u32[]{:S(2)}) %all-to-all-start) | async-done | bytes 1048608 | tf_op jit(solution)/shard_map/all_to_all | solution.py:174
  57.4 41.7 %all-to-all-done.2 = f32[1,8,32,2048]{3,2,0,1:T(8,128)S(1)} async-done(((f32[1,8,32,2048]{3,2,0,1:T(8,128)}), f32[1,8,32,2048]{3,2,0,1:T(8,128)S(1)}, u32[]{:S(2)}, u32[]{:S(2)}) %all-to-all-start.2) | async-done | bytes 2097184 | tf_op jit(solution)/shard_map/all_to_all | solution.py:100
  103.7 114.4 %while.39 = (s32[]{:T(128)}, f32[4,64,2048]{2,1,0:T(8,128)}, f32[4,64,2048]{2,1,0:T(8,128)}, f32[4,64,2048]{2,1,0:T(8,128)}, f32[4,64,2048]{2,1,0:T(8,128)}, /*i...) while((s32[]{:T(128)}, f32[4,64,2048]{2,1,0:T(8,128)}, ...), condition=%wide.region_5.6_spmd, body=%wide.region_0.5_spmd.sunk | while | flops 70910216 | bytes 10621447 | solution.py:169
  115.0 15.1 %fusion.311 = (f32[64,2048]{1,0:T(8,128)S(1)}, f32[64,2048]{1,0:T(8,128)S(1)}, f32[64,2048]{1,0:T(8,128)S(1)}, f32[64,2048]{1,0:T(8,128)S(1)}) fusion(f32[64]{0:T(128)S(1)} %get-tuple-element.924, f32[64]{0:T(128)S(1)} %get-tuple-element.925, f32[2048,16]{0,1:T(8,128)S(1)} %get-tuple-element.1023, f32[2048,16]{0,1:T(8,128)S(1)} %copy.198, ...), kind=kLoop, calls=%fused_computation.19.clone.1 | loop fusion | flops 70778880 | bytes 2884736 | tf_op jit(solution)/shard_map/while/body/eval_jaxpr/reduce_sum | solution.py:165
  143.7 15.1 %fusion.311 = (f32[64,2048]{1,0:T(8,128)S(1)}, f32[64,2048]{1,0:T(8,128)S(1)}, f32[64,2048]{1,0:T(8,128)S(1)}, f32[64,2048]{1,0:T(8,128)S(1)}) fusion(f32[64]{0:T(128)S(1)} %get-tuple-element.924, f32[64]{0:T(128)S(1)} %get-tuple-element.925, f32[2048,16]{0,1:T(8,128)S(1)} %get-tuple-element.1023, f32[2048,16]{0,1:T(8,128)S(1)} %copy.198, ...), kind=kLoop, calls=%fused_computation.19.clone.1 | loop fusion | flops 70778880 | bytes 2884736 | tf_op jit(solution)/shard_map/while/body/eval_jaxpr/reduce_sum | solution.py:165
  172.2 15.1 %fusion.311 = (f32[64,2048]{1,0:T(8,128)S(1)}, f32[64,2048]{1,0:T(8,128)S(1)}, f32[64,2048]{1,0:T(8,128)S(1)}, f32[64,2048]{1,0:T(8,128)S(1)}) fusion(f32[64]{0:T(128)S(1)} %get-tuple-element.924, f32[64]{0:T(128)S(1)} %get-tuple-element.925, f32[2048,16]{0,1:T(8,128)S(1)} %get-tuple-element.1023, f32[2048,16]{0,1:T(8,128)S(1)} %copy.198, ...), kind=kLoop, calls=%fused_computation.19.clone.1 | loop fusion | flops 70778880 | bytes 2884736 | tf_op jit(solution)/shard_map/while/body/eval_jaxpr/reduce_sum | solution.py:165
  200.8 15.1 %fusion.311 = (f32[64,2048]{1,0:T(8,128)S(1)}, f32[64,2048]{1,0:T(8,128)S(1)}, f32[64,2048]{1,0:T(8,128)S(1)}, f32[64,2048]{1,0:T(8,128)S(1)}) fusion(f32[64]{0:T(128)S(1)} %get-tuple-element.924, f32[64]{0:T(128)S(1)} %get-tuple-element.925, f32[2048,16]{0,1:T(8,128)S(1)} %get-tuple-element.1023, f32[2048,16]{0,1:T(8,128)S(1)} %copy.198, ...), kind=kLoop, calls=%fused_computation.19.clone.1 | loop fusion | flops 70778880 | bytes 2884736 | tf_op jit(solution)/shard_map/while/body/eval_jaxpr/reduce_sum | solution.py:165
  241.9 8.5 multiply_subtract_fusion.2
  250.4 9.0 multiply_add_fusion.6
  283.2 37.7 %all-to-all-done.3 = f32[1,8,32,2048]{3,2,0,1:T(8,128)} async-done(((f32[1,8,32,2048]{3,2,0,1:T(8,128)}), f32[1,8,32,2048]{3,2,0,1:T(8,128)}, u32[]{:S(2)}, u32[]{:S(2)}) %all-to-all-start.3) | async-done | bytes 2097184 | tf_op jit(solution)/shard_map/all_to_all | solution.py:127
  331.2 42.2 %all-to-all-done.4 = f32[1,8,32,2048]{3,2,0,1:T(8,128)S(1)} async-done(((f32[1,8,32,2048]{3,2,0,1:T(8,128)}), f32[1,8,32,2048]{3,2,0,1:T(8,128)S(1)}, u32[]{:S(2)}, u32[]{:S(2)}) %all-to-all-start.4) | async-done | bytes 2097184 | tf_op jit(solution)/shard_map/all_to_all | solution.py:128
  379.5 51.9 %all_to_all.60 = f32[1,8,32,2048]{3,2,0,1:T(8,128)S(1)} all-to-all(f32[1,8,32,2048]{3,2,0,1:T(8,128)S(1)} %copy.131), channel_id=1, replica_groups=mesh['ctx'=8,'chan'=2,'dp'=2] {'ctx'}, dimensions={1} | all-to-all | bytes 4194304 | tf_op jit(solution)/shard_map/all_to_all | solution.py:183
  442.8 52.1 %all_to_all.61 = f32[1,8,32,2048]{3,2,0,1:T(8,128)S(1)} all-to-all(f32[1,8,32,2048]{3,2,0,1:T(8,128)S(1)} %bitcast.214), channel_id=1, replica_groups=mesh['ctx'=8,'chan'=2,'dp'=2] {'ctx'}, dimensions={1} | all-to-all | bytes 4194304 | tf_op jit(solution)/shard_map/all_to_all | solution.py:187
  510.9 41.6 %all-to-all-done.8 = f32[1,8,32,2048]{3,2,0,1:T(8,128)} async-done(((f32[1,8,32,2048]{3,2,0,1:T(8,128)}), f32[1,8,32,2048]{3,2,0,1:T(8,128)}, u32[]{:S(2)}, u32[]{:S(2)}) %all-to-all-start.8) | async-done | bytes 2097184 | tf_op jit(solution)/shard_map/all_to_all | solution.py:100
  556.3 7.2 convolution_bitcast_fusion
  563.5 7.3 convolution_bitcast_fusion.1
  570.8 33.8 %all-to-all-done.7 = f32[1,8,32,2048]{3,2,0,1:T(8,128)S(1)} async-done(((f32[1,8,32,2048]{3,2,0,1:T(8,128)}), f32[1,8,32,2048]{3,2,0,1:T(8,128)S(1)}, u32[]{:S(2)}, u32[]{:S(2)}) %all-to-all-start.7) | async-done | bytes 2097184 | tf_op jit(solution)/shard_map/all_to_all | solution.py:99
  610.4 18.4 %subtract_bitcast_fusion.1 = (f32[256,2048]{0,1:T(8,128)}, f32[256,2048]{0,1:T(8,128)}, f32[256,2048]{0,1:T(8,128)}, f32[256,2048]{0,1:T(8,128)}, f32[1,256,2048...) fusion(f32[1,256,2048]{1,2,0:T(8,128)} %copy-done.9, ...), kind=kOutput, calls=%fused_computation.170 | convolution fusion | flops 1630928896 | bytes 41944064 | tf_op jit(solution)/shard_map/kj,xjc->xkc/dot_general | solution.py:104
  651.4 37.5 %all-to-all-done.9 = f32[1,8,32,2048]{3,2,0,1:T(8,128)} async-done(((f32[1,8,32,2048]{3,2,0,1:T(8,128)}), f32[1,8,32,2048]{3,2,0,1:T(8,128)}, u32[]{:S(2)}, u32[]{:S(2)}) %all-to-all-start.9) | async-done | bytes 2097184 | tf_op jit(solution)/shard_map/all_to_all | solution.py:127
  709.6 31.7 %all-to-all-done.10 = f32[1,8,32,2048]{3,2,0,1:T(8,128)} async-done(((f32[1,8,32,2048]{3,2,0,1:T(8,128)}), f32[1,8,32,2048]{3,2,0,1:T(8,128)}, u32[]{:S(2)}, u32[]{:S(2)}) %all-to-all-start.10) | async-done | bytes 2097184 | tf_op jit(solution)/shard_map/all_to_all | solution.py:128
  754.4 203.1 %while.40 = (s32[]{:T(128)}, f32[2048,16]{0,1:T(8,128)}, f32[2048,16]{0,1:T(8,128)}, f32[2048,16]{0,1:T(8,128)}, f32[2048,16]{0,1:T(8,128)}, /*index=5*/s32[4]{0...) while((s32[]{:T(128)}, f32[2048,16]{0,1:T(8,128)}, ...), condition=%wide.region_15.16_spmd.clone, body=%wide.region_10.15_spmd.clone.sunk | while | flops 180650240 | bytes 40907724 | solution.py:252
  772.9 13.5 %add_reduce_fusion.8 = (f32[2048,16]{0,1:T(8,128)S(1)}, f32[2048,16]{0,1:T(8,128)S(1)}) fusion(f32[64]{0:T(128)S(1)} %get-tuple-element.967, f32[64,2048]{1,0:T(8,128)S(1)} %copy-done, f32[64]{0:T(128)S(1)} %get-tuple-element.968, f32[64]{0:T(128)S(1)} %get-tuple-element.969, f32[64,2048]{1,0:T(8,128)S(1)} %copy-done.1, f32[2048,16]{0,1:T(8,128)S(1)} %copy.203, ...), kind=kLoop, calls=%fused_computation.71.clone.1 | loop fusion | flops 90112000 | bytes 2360128 | tf_op jit(solution)/shard_map/while/body/eval_jaxpr/reduce_sum | solution.py:243
  790.3 12.9 %add_reduce_fusion.7 = (f32[2048,16]{0,1:T(8,128)S(1)}, f32[2048,16]{0,1:T(8,128)S(1)}) fusion(f32[2048,16]{0,1:T(8,128)S(1)} %copy.203, f32[64]{0:T(128)S(1)} %get-tuple-element.956, f32[2048,16]{0,1:T(8,128)S(1)} %copy.204, f32[2048,16]{0,1:T(8,128)S(1)} %copy.205, f32[64,2048]{1,0:T(8,128)S(1)} %constant_dynamic-slice_fusion.8, ...), kind=kLoop, calls=%fused_computation.75.clone.1 | loop fusion | flops 90112000 | bytes 2360128 | tf_op jit(solution)/shard_map/while/body/eval_jaxpr/reduce_sum | solution.py:243
  822.9 13.5 %add_reduce_fusion.8 = (f32[2048,16]{0,1:T(8,128)S(1)}, f32[2048,16]{0,1:T(8,128)S(1)}) fusion(f32[64]{0:T(128)S(1)} %get-tuple-element.967, f32[64,2048]{1,0:T(8,128)S(1)} %copy-done, f32[64]{0:T(128)S(1)} %get-tuple-element.968, f32[64]{0:T(128)S(1)} %get-tuple-element.969, f32[64,2048]{1,0:T(8,128)S(1)} %copy-done.1, f32[2048,16]{0,1:T(8,128)S(1)} %copy.203, ...), kind=kLoop, calls=%fused_computation.71.clone.1 | loop fusion | flops 90112000 | bytes 2360128 | tf_op jit(solution)/shard_map/while/body/eval_jaxpr/reduce_sum | solution.py:243
  841.2 12.9 %add_reduce_fusion.7 = (f32[2048,16]{0,1:T(8,128)S(1)}, f32[2048,16]{0,1:T(8,128)S(1)}) fusion(f32[2048,16]{0,1:T(8,128)S(1)} %copy.203, f32[64]{0:T(128)S(1)} %get-tuple-element.956, f32[2048,16]{0,1:T(8,128)S(1)} %copy.204, f32[2048,16]{0,1:T(8,128)S(1)} %copy.205, f32[64,2048]{1,0:T(8,128)S(1)} %constant_dynamic-slice_fusion.8, ...), kind=kLoop, calls=%fused_computation.75.clone.1 | loop fusion | flops 90112000 | bytes 2360128 | tf_op jit(solution)/shard_map/while/body/eval_jaxpr/reduce_sum | solution.py:243
  873.9 13.5 %add_reduce_fusion.8 = (f32[2048,16]{0,1:T(8,128)S(1)}, f32[2048,16]{0,1:T(8,128)S(1)}) fusion(f32[64]{0:T(128)S(1)} %get-tuple-element.967, f32[64,2048]{1,0:T(8,128)S(1)} %copy-done, f32[64]{0:T(128)S(1)} %get-tuple-element.968, f32[64]{0:T(128)S(1)} %get-tuple-element.969, f32[64,2048]{1,0:T(8,128)S(1)} %copy-done.1, f32[2048,16]{0,1:T(8,128)S(1)} %copy.203, ...), kind=kLoop, calls=%fused_computation.71.clone.1 | loop fusion | flops 90112000 | bytes 2360128 | tf_op jit(solution)/shard_map/while/body/eval_jaxpr/reduce_sum | solution.py:243
  892.2 12.9 %add_reduce_fusion.7 = (f32[2048,16]{0,1:T(8,128)S(1)}, f32[2048,16]{0,1:T(8,128)S(1)}) fusion(f32[2048,16]{0,1:T(8,128)S(1)} %copy.203, f32[64]{0:T(128)S(1)} %get-tuple-element.956, f32[2048,16]{0,1:T(8,128)S(1)} %copy.204, f32[2048,16]{0,1:T(8,128)S(1)} %copy.205, f32[64,2048]{1,0:T(8,128)S(1)} %constant_dynamic-slice_fusion.8, ...), kind=kLoop, calls=%fused_computation.75.clone.1 | loop fusion | flops 90112000 | bytes 2360128 | tf_op jit(solution)/shard_map/while/body/eval_jaxpr/reduce_sum | solution.py:243
  924.8 13.5 %add_reduce_fusion.8 = (f32[2048,16]{0,1:T(8,128)S(1)}, f32[2048,16]{0,1:T(8,128)S(1)}) fusion(f32[64]{0:T(128)S(1)} %get-tuple-element.967, f32[64,2048]{1,0:T(8,128)S(1)} %copy-done, f32[64]{0:T(128)S(1)} %get-tuple-element.968, f32[64]{0:T(128)S(1)} %get-tuple-element.969, f32[64,2048]{1,0:T(8,128)S(1)} %copy-done.1, f32[2048,16]{0,1:T(8,128)S(1)} %copy.203, ...), kind=kLoop, calls=%fused_computation.71.clone.1 | loop fusion | flops 90112000 | bytes 2360128 | tf_op jit(solution)/shard_map/while/body/eval_jaxpr/reduce_sum | solution.py:243
  943.1 12.9 %add_reduce_fusion.7 = (f32[2048,16]{0,1:T(8,128)S(1)}, f32[2048,16]{0,1:T(8,128)S(1)}) fusion(f32[2048,16]{0,1:T(8,128)S(1)} %copy.203, f32[64]{0:T(128)S(1)} %get-tuple-element.956, f32[2048,16]{0,1:T(8,128)S(1)} %copy.204, f32[2048,16]{0,1:T(8,128)S(1)} %copy.205, f32[64,2048]{1,0:T(8,128)S(1)} %constant_dynamic-slice_fusion.8, ...), kind=kLoop, calls=%fused_computation.75.clone.1 | loop fusion | flops 90112000 | bytes 2360128 | tf_op jit(solution)/shard_map/while/body/eval_jaxpr/reduce_sum | solution.py:243
  966.1 22.5 %psum.63 = f32[2048]{0:T(1024)} all-reduce(f32[2048]{0:T(1024)S(1)} %psum.62), channel_id=1, replica_groups=mesh['ctx'=8,'chan'=2,'dp'=2] {'ctx'}, use_global_device_ids=true, to_apply=%region_22.23 | all-reduce | flops 2048 | bytes 16384 | tf_op jit(solution)/shard_map/psum | solution.py:263
  992.5 68.1 %all-reduce.5.cloned.1.call-done = (f32[2048,16]{0,1:T(8,128)}, f32[2048,16]{0,1:T(8,128)}) async-done(((f32[2048,16]{0,1:T(8,128)}, f32[2048,16]{0,1:T(8,128)}), (f32[2048,16]{0,1:T(8,128)}, f32[2048,16]{0,1:T(8,128)})) %all-reduce.5.cloned.1.call-update) | async-done | bytes 262160 | tf_op jit(solution)/shard_map/psum | solution.py:263
  (461 shorter events, 340.4 us)
Async XLA Ops:
  10.1 33.0 %all-to-all-start = ((bf16[1,8,32,2048]{3,2,0,1:T(8,128)(2,1)}), bf16[1,8,32,2048]{3,2,0,1:T(8,128)(2,1)S(1)}, u32[]{:S(2)}, u32[]{:S(2)}) async-start(bf16[1,8,32,2048]{3,2,0,1:T(8,128)(2,1)} %bitcast.6), calls=%async_computation | async-start | bytes 2097152 | tf_op jit(solution)/shard_map/all_to_all | solution.py:174
  47.1 52.0 %all-to-all-start.2 = ((f32[1,8,32,2048]{3,2,0,1:T(8,128)}), f32[1,8,32,2048]{3,2,0,1:T(8,128)S(1)}, u32[]{:S(2)}, u32[]{:S(2)}) async-start(f32[1,8,32,2048]{3,2,0,1:T(8,128)} %copy.120), calls=%async_computation.2 | async-start | bytes 4194304 | tf_op jit(solution)/shard_map/all_to_all | solution.py:100
  57.4 46.3 %copy-start.27 = (f32[2048,16]{0,1:T(8,128)S(1)}, f32[2048,16]{0,1:T(8,128)}, u32[]{:S(2)}) copy-start(f32[2048,16]{0,1:T(8,128)} %param.16) | copy-start | bytes 393220
  99.1 136.0 %all-to-all-start.1 = ((f32[1,8,32,2048]{3,2,0,1:T(8,128)}), f32[1,8,32,2048]{3,2,0,1:T(8,128)}, u32[]{:S(2)}, u32[]{:S(2)}) async-start(f32[1,8,32,2048]{3,2,0,1:T(8,128)} %copy.116), calls=%async_computation.1 | async-start | bytes 4194304 | tf_op jit(solution)/shard_map/all_to_all | solution.py:99
  267.5 53.4 %all-to-all-start.3 = ((f32[1,8,32,2048]{3,2,0,1:T(8,128)}), f32[1,8,32,2048]{3,2,0,1:T(8,128)}, u32[]{:S(2)}, u32[]{:S(2)}) async-start(f32[1,8,32,2048]{3,2,0,1:T(8,128)} %bitcast.213), calls=%async_computation.3 | async-start | bytes 4194304 | tf_op jit(solution)/shard_map/all_to_all | solution.py:127
  320.9 52.4 %all-to-all-start.4 = ((f32[1,8,32,2048]{3,2,0,1:T(8,128)}), f32[1,8,32,2048]{3,2,0,1:T(8,128)S(1)}, u32[]{:S(2)}, u32[]{:S(2)}) async-start(f32[1,8,32,2048]{3,2,0,1:T(8,128)} %bitcast.44), calls=%async_computation.4 | async-start | bytes 4194304 | tf_op jit(solution)/shard_map/all_to_all | solution.py:128
  379.5 52.0 %copy-start.25 = (bf16[1,256,2048]{2,1,0:T(8,128)(2,1)S(1)}, bf16[1,256,2048]{2,1,0:T(8,128)(2,1)}, u32[]{:S(2)}) copy-start(bf16[1,256,2048]{2,1,0:T(8,128)(2,1)} %param.11) | copy-start | bytes 3145732
  500.7 51.8 %all-to-all-start.8 = ((f32[1,8,32,2048]{3,2,0,1:T(8,128)}), f32[1,8,32,2048]{3,2,0,1:T(8,128)}, u32[]{:S(2)}, u32[]{:S(2)}) async-start(f32[1,8,32,2048]{3,2,0,1:T(8,128)} %copy.137), calls=%async_computation.8 | async-start | bytes 4194304 | tf_op jit(solution)/shard_map/all_to_all | solution.py:100
  552.5 52.0 %all-to-all-start.7 = ((f32[1,8,32,2048]{3,2,0,1:T(8,128)}), f32[1,8,32,2048]{3,2,0,1:T(8,128)S(1)}, u32[]{:S(2)}, u32[]{:S(2)}) async-start(f32[1,8,32,2048]{3,2,0,1:T(8,128)} %copy.134), calls=%async_computation.7 | async-start | bytes 4194304 | tf_op jit(solution)/shard_map/all_to_all | solution.py:99
  636.6 52.3 %all-to-all-start.9 = ((f32[1,8,32,2048]{3,2,0,1:T(8,128)}), f32[1,8,32,2048]{3,2,0,1:T(8,128)}, u32[]{:S(2)}, u32[]{:S(2)}) async-start(f32[1,8,32,2048]{3,2,0,1:T(8,128)} %bitcast.212), calls=%async_computation.9 | async-start | bytes 4194304 | tf_op jit(solution)/shard_map/all_to_all | solution.py:127
  689.0 52.4 %all-to-all-start.10 = ((f32[1,8,32,2048]{3,2,0,1:T(8,128)}), f32[1,8,32,2048]{3,2,0,1:T(8,128)}, u32[]{:S(2)}, u32[]{:S(2)}) async-start(f32[1,8,32,2048]{3,2,0,1:T(8,128)} %bitcast.211), calls=%async_computation.10 | async-start | bytes 4194304 | tf_op jit(solution)/shard_map/all_to_all | solution.py:128
  749.4 239.3 %all-to-all-start.11 = ((f32[1,8,32,2048]{3,2,0,1:T(8,128)}), f32[1,8,32,2048]{3,2,0,1:T(8,128)}, u32[]{:S(2)}, u32[]{:S(2)}) async-start(f32[1,8,32,2048]{3,2,0,1:T(8,128)} %copy.148), calls=%async_computation.11 | async-start | bytes 4194304 | tf_op jit(solution)/shard_map/all_to_all | solution.py:196
  753.7 234.9 %all-reduce.7.cloned.1.call-start = ((), (), s32[]{:S(2)}) async-start(), calls=%async_computation.13 | async-start | bytes 524288 | tf_op jit(solution)/shard_map/psum | solution.py:264
  772.3 14.2 %copy-start.33 = (f32[2048,16]{0,1:T(8,128)S(1)}, f32[2048,16]{0,1:T(8,128)}, u32[]{:S(2)}) copy-start(f32[2048,16]{0,1:T(8,128)} %get-tuple-element.1057) | copy-start | bytes 393220 | tf_op jit(solution)/shard_map/while
  772.9 14.3 %copy-start.39 = (f32[256]{0:T(256)S(1)}, f32[256]{0:T(256)}, u32[]{:S(2)}) copy-start(f32[256]{0:T(256)} %get-tuple-element.1088) | copy-start | bytes 3076 | tf_op jit(solution)/shard_map/while
  787.9 15.4 %copy-start.29 = (f32[2048,16]{0,1:T(8,128)S(1)}, f32[2048,16]{0,1:T(8,128)}, u32[]{:S(2)}) copy-start(f32[2048,16]{0,1:T(8,128)} %get-tuple-element.1055) | copy-start | bytes 393220 | tf_op jit(solution)/shard_map/while
  787.9 15.4 %copy-start.31 = (f32[2048,16]{0,1:T(8,128)S(1)}, f32[2048,16]{0,1:T(8,128)}, u32[]{:S(2)}) copy-start(f32[2048,16]{0,1:T(8,128)} %get-tuple-element.1056) | copy-start | bytes 393220 | tf_op jit(solution)/shard_map/while
  789.0 15.7 %copy-start.24 = (f32[256,2048]{1,0:T(8,128)S(1)}, f32[256,2048]{1,0:T(8,128)}, u32[]{:S(2)}) copy-start(f32[256,2048]{1,0:T(8,128)} %copy-done.23) | copy-start | bytes 6291460 | tf_op jit(solution)/shard_map/while
  822.9 15.2 %copy-start.39 = (f32[256]{0:T(256)S(1)}, f32[256]{0:T(256)}, u32[]{:S(2)}) copy-start(f32[256]{0:T(256)} %get-tuple-element.1088) | copy-start | bytes 3076 | tf_op jit(solution)/shard_map/while
  838.8 15.4 %copy-start.29 = (f32[2048,16]{0,1:T(8,128)S(1)}, f32[2048,16]{0,1:T(8,128)}, u32[]{:S(2)}) copy-start(f32[2048,16]{0,1:T(8,128)} %get-tuple-element.1055) | copy-start | bytes 393220 | tf_op jit(solution)/shard_map/while
  838.8 15.4 %copy-start.31 = (f32[2048,16]{0,1:T(8,128)S(1)}, f32[2048,16]{0,1:T(8,128)}, u32[]{:S(2)}) copy-start(f32[2048,16]{0,1:T(8,128)} %get-tuple-element.1056) | copy-start | bytes 393220 | tf_op jit(solution)/shard_map/while
  839.9 15.7 %copy-start.24 = (f32[256,2048]{1,0:T(8,128)S(1)}, f32[256,2048]{1,0:T(8,128)}, u32[]{:S(2)}) copy-start(f32[256,2048]{1,0:T(8,128)} %copy-done.23) | copy-start | bytes 6291460 | tf_op jit(solution)/shard_map/while
  873.9 15.2 %copy-start.39 = (f32[256]{0:T(256)S(1)}, f32[256]{0:T(256)}, u32[]{:S(2)}) copy-start(f32[256]{0:T(256)} %get-tuple-element.1088) | copy-start | bytes 3076 | tf_op jit(solution)/shard_map/while
  889.7 15.4 %copy-start.29 = (f32[2048,16]{0,1:T(8,128)S(1)}, f32[2048,16]{0,1:T(8,128)}, u32[]{:S(2)}) copy-start(f32[2048,16]{0,1:T(8,128)} %get-tuple-element.1055) | copy-start | bytes 393220 | tf_op jit(solution)/shard_map/while
  889.7 15.4 %copy-start.31 = (f32[2048,16]{0,1:T(8,128)S(1)}, f32[2048,16]{0,1:T(8,128)}, u32[]{:S(2)}) copy-start(f32[2048,16]{0,1:T(8,128)} %get-tuple-element.1056) | copy-start | bytes 393220 | tf_op jit(solution)/shard_map/while
  890.8 15.7 %copy-start.24 = (f32[256,2048]{1,0:T(8,128)S(1)}, f32[256,2048]{1,0:T(8,128)}, u32[]{:S(2)}) copy-start(f32[256,2048]{1,0:T(8,128)} %copy-done.23) | copy-start | bytes 6291460 | tf_op jit(solution)/shard_map/while
  924.8 15.2 %copy-start.39 = (f32[256]{0:T(256)S(1)}, f32[256]{0:T(256)}, u32[]{:S(2)}) copy-start(f32[256]{0:T(256)} %get-tuple-element.1088) | copy-start | bytes 3076 | tf_op jit(solution)/shard_map/while
  940.6 15.4 %copy-start.29 = (f32[2048,16]{0,1:T(8,128)S(1)}, f32[2048,16]{0,1:T(8,128)}, u32[]{:S(2)}) copy-start(f32[2048,16]{0,1:T(8,128)} %get-tuple-element.1055) | copy-start | bytes 393220 | tf_op jit(solution)/shard_map/while
  940.6 15.4 %copy-start.31 = (f32[2048,16]{0,1:T(8,128)S(1)}, f32[2048,16]{0,1:T(8,128)}, u32[]{:S(2)}) copy-start(f32[2048,16]{0,1:T(8,128)} %get-tuple-element.1056) | copy-start | bytes 393220 | tf_op jit(solution)/shard_map/while
  941.8 15.7 %copy-start.24 = (f32[256,2048]{1,0:T(8,128)S(1)}, f32[256,2048]{1,0:T(8,128)}, u32[]{:S(2)}) copy-start(f32[256,2048]{1,0:T(8,128)} %copy-done.23) | copy-start | bytes 6291460 | tf_op jit(solution)/shard_map/while
  957.4 31.3 %copy-start.35 = (bf16[1,256,2048]{2,1,0:T(8,128)(2,1)S(1)}, bf16[1,256,2048]{2,1,0:T(8,128)(2,1)}, u32[]{:S(2)}) copy-start(bf16[1,256,2048]{2,1,0:T(8,128)(2,1)} %param.13) | copy-start | bytes 3145732
  961.0 99.6 %all-reduce.5.cloned.1.call-start = ((), (), s32[]{:S(2)}) async-start(), calls=%async_computation.12 | async-start | bytes 524288 | tf_op jit(solution)/shard_map/psum | solution.py:263
  (65 other events, 272.6 us)
Sparse Core Ops, SparseCore 0:
  961.1 24.6 all-reduce.6
  989.6 70.8 all-reduce.4
